TPU v7x, 32 devices: a whole 2x2x4 slice. The times are simulated.
32 devices in a mesh: batch: 1, wide: 32 (over z, y, x, core).
Axes of the slice: x: 2, y: 2, z: 4, core: 2. Of those that a mesh axis runs over, the one named last changes fastest.
Arguments:
- features: bfloat16 [64, 64, 1, 1024], P('wide', None, 'batch'), may hold values from -6 to 6
- conv_weight: bfloat16 [3, 3, 32, 1024], replicated, may hold values from -0.375 to 0.375
- proj_weight: bfloat16 [1024, 128], replicated, may hold values from -0.1875 to 0.1875
- anchor_pixel: int32 [512, 1], P('wide', 'batch'), may hold values from 0 to 127
- positive_pixel: int32 [512, 1], P('wide', 'batch'), may hold values from 0 to 4095
Outputs:
- grad_features: bfloat16 [64, 64, 1, 1024], P('wide', None, 'batch')
- grad_conv: float32 [3, 3, 32, 1024], replicated
- grad_proj: float32 [1024, 128], replicated
- loss_value: float32 [], replicated
Inputs may be any that keep to these rules, and one draw needn't show every extreme that they name: anchor_pixel[n, b] names a pixel of row tile n // 16. positive_pixel names a pixel of the same image as the anchor.
All inputs are finite; a program needn't handle non-finite values.
Results may differ from a plain program's by a relative error of at most 0.01.
Values may be sent and summed in bfloat16 or wider, within the bound.
A program may use at most 64 MiB of HBM per device.

v0:
```python
import functools

import jax
import jax.numpy as jnp
from jax import lax
from jax.experimental import pallas as pl
from jax.experimental.pallas import tpu as pltpu
from jax.sharding import PartitionSpec as P

SOFTMAX_TEMPER = 0.1
EPSILON = 1e-06
LANES = 128
F32 = jnp.float32
BF16 = jnp.bfloat16
MESH = pl.DeviceIdType.MESH

NN = (((1,), (0,)), ((), ()))
NT = (((1,), (1,)), ((), ()))
TN = (((0,), (0,)), ((), ()))


def mm(a, b, dims, precision=None):
    return lax.dot_general(a, b, dims, preferred_element_type=F32, precision=precision)


def iota(shape, dim):
    return lax.broadcasted_iota(jnp.int32, shape, dim)


def store_shifted(dst, rows, start, values, cols):
    wide = values.astype(F32)
    count = wide.shape[0]
    col = iota(wide.shape, 0) % cols
    dst[1, start : start + rows] = values
    left = jnp.where(col == 0, 0.0, pltpu.roll(wide, 1, 0))
    dst[0, start : start + rows] = left.astype(BF16)
    right = jnp.where(col == cols - 1, 0.0, pltpu.roll(wide, count - 1, 0))
    dst[2, start : start + rows] = right.astype(BF16)


def kernel(
    devices,
    anchors_all,
    gradient_scale,
    geometry,
    x_ref,
    w_ref,
    proj_ref,
    anchor_ref,
    positive_ref,
    out_ref,
    ag,
    loss_ref,
    xh,
    xs,
    wn,
    wt,
    at,
    mixed,
    mixed_t,
    slope,
    posb,
    qall,
    totp,
    totx,
    totb,
    wps,
    wpx,
    wpc,
    wpr,
    gm,
    gp,
    gh,
    gs,
    gw,
    gpj,
    l1s,
    l1r,
    l2s,
    l2r,
    xh_send,
    xh_recv,
    gh_send,
    gh_recv,
    pos_send,
    pos_recv,
    q_send,
    q_recv,
    tot_send,
    tot_recv,
    wp_send,
    wp_recv,
    totx_send,
    totx_recv,
    wpx_send,
    wpx_recv,
    l1_send,
    l1_recv,
    l2_send,
    l2_recv,
    ag_send,
    near_send,
    ag_recv,
    pair_send,
    pair_recv,
):
    cols, group, pieces, piece, prow, inner, anchor_count = geometry
    pixels, channels = x_ref.shape
    blocks = channels // LANES
    per_block = LANES // group
    anchors_dev = anchor_ref.shape[1]
    chips = devices // 2
    me = lax.axis_index("wide")
    core = lax.rem(me, 2)
    chip = me // 2
    partner = me + 1 - 2 * core
    barrier = pltpu.get_barrier_semaphore()

    def others(body):
        def step(k, carry):
            body(lax.rem(me + k, devices))
            return carry

        lax.fori_loop(1, devices, step, 0)

    def other_chips(body):
        def step(k, carry):
            body(lax.rem(chip + k, chips))
            return carry

        lax.fori_loop(1, chips, step, 0)

    def remote(src, dst, send_sem, recv_sem, target):
        return pltpu.make_async_remote_copy(
            src_ref=src,
            dst_ref=dst,
            send_sem=send_sem,
            recv_sem=recv_sem,
            device_id={"wide": target},
            device_id_type=MESH,
        )

    def signal_entry(target):
        pl.semaphore_signal(barrier, inc=1, device_id={"wide": target}, device_id_type=MESH)

    others(signal_entry)

    tap_count = w_ref.shape[0]
    diagonal = iota((LANES, LANES), 0) // group == iota((LANES, LANES), 1) // group

    def build(b, carry):
        lane = pl.ds(pl.multiple_of(b * LANES, LANES), LANES)
        for tap in range(tap_count):
            slab = w_ref[tap, :, lane].astype(F32)
            full = jnp.where(diagonal, jnp.concatenate([slab] * per_block, axis=0), 0.0)
            full = full.astype(BF16)
            wn[b, tap * LANES : (tap + 1) * LANES, :] = full
            wt[b, :, tap * LANES : (tap + 1) * LANES] = full
        return carry

    lax.fori_loop(0, blocks, build, 0)
    store_shifted(xs, pixels, cols, x_ref[...], cols)

    posb[me, :, :anchors_dev] = positive_ref[...].astype(F32)
    posb[me, :, anchors_dev:] = jnp.zeros((1, LANES - anchors_dev), F32)
    eye = iota((anchors_dev, anchors_dev), 0) == iota((anchors_dev, anchors_dev), 1)
    anchor_col = jnp.sum(
        jnp.where(eye, anchor_ref[...].astype(F32), 0.0), axis=1, keepdims=True
    )

    pl.semaphore_wait(barrier, devices - 1)

    has_prev = me > 0
    has_next = me < devices - 1
    previous = lax.rem(me + devices - 1, devices)
    following = lax.rem(me + 1, devices)

    def halo(src, buf, send_sem, recv_sem):
        up = remote(
            src.at[pl.ds(0, cols)], buf.at[1], send_sem.at[0], recv_sem.at[1], previous
        )
        down = remote(
            src.at[pl.ds(pixels - cols, cols)],
            buf.at[0],
            send_sem.at[1],
            recv_sem.at[0],
            following,
        )
        return up, down

    def halo_start(copies):
        up, down = copies

        @pl.when(has_prev)
        def _():
            up.start()

        @pl.when(has_next)
        def _():
            down.start()

    def halo_wait(copies, buf):
        up, down = copies

        @pl.when(has_prev)
        def _():
            up.wait_send()
            down.wait_recv()

        @pl.when(jnp.logical_not(has_prev))
        def _():
            buf[0] = jnp.zeros(buf.shape[1:], buf.dtype)

        @pl.when(has_next)
        def _():
            down.wait_send()
            up.wait_recv()

        @pl.when(jnp.logical_not(has_next))
        def _():
            buf[1] = jnp.zeros(buf.shape[1:], buf.dtype)

    def to_all(buf, send_sem, recv_sem):
        def go(target):
            remote(
                buf.at[me], buf.at[me], send_sem.at[target], recv_sem.at[me], target
            ).start()

        return go

    def from_all(buf, send_sem, recv_sem):
        def done(source):
            copy = remote(
                buf.at[source], buf.at[source], send_sem.at[source], recv_sem.at[source], source
            )
            copy.wait_recv()
            copy.wait_send()

        return done

    x_halo = halo(x_ref, xh, xh_send, xh_recv)
    halo_start(x_halo)
    others(to_all(posb, pos_send, pos_recv))
    halo_wait(x_halo, xh)
    store_shifted(xs, cols, 0, xh[0], cols)
    store_shifted(xs, cols, cols + pixels, xh[1], cols)

    def windows(buf, lane, flip):
        parts = []
        for row in range(3):
            for col in range(3):
                r, c = (2 - row, 2 - col) if flip else (row, col)
                parts.append(buf[c, r * cols : r * cols + pixels, lane])
        return jnp.concatenate(parts, axis=1)

    def forward(b, carry):
        lane = pl.ds(pl.multiple_of(b * LANES, LANES), LANES)
        pre = mm(windows(xs, lane, False), wn[b], NN)
        sig = 1.0 / (1.0 + jnp.exp(-pre))
        mixed[:, lane] = (x_ref[:, lane].astype(F32) + pre * sig).astype(BF16)
        slope[:, lane] = sig * (1.0 + pre * (1.0 - sig))
        return carry

    lax.fori_loop(0, blocks, forward, 0)

    raw_key = mm(mixed[...], proj_ref[...], NN)
    norm_key = jnp.sqrt(jnp.sum(raw_key * raw_key, axis=1, keepdims=True) + EPSILON)
    unit_key = raw_key / norm_key
    keys = unit_key.astype(BF16)
    pick = jnp.where(
        iota((anchors_dev, pixels), 1).astype(F32) == anchor_col, 1.0, 0.0
    )
    qall[me] = mm(pick.astype(BF16), keys, NN).astype(BF16)
    others(to_all(qall, q_send, q_recv))

    def flip_over(b, carry):
        start = pl.multiple_of(b * LANES, LANES)
        lane = pl.ds(start, LANES)
        at[b] = windows(xs, lane, False).T
        mixed_t[lane, :] = mixed[:, lane].T
        return carry

    lax.fori_loop(0, blocks, flip_over, 0)

    others(from_all(posb, pos_send, pos_recv))
    own_lane = iota((devices, anchors_dev, LANES), 1) == iota((devices, anchors_dev, LANES), 2)
    pos_all = jnp.sum(jnp.where(own_lane, posb[...], 0.0), axis=2, keepdims=True)
    pos_local = pos_all - (me * pixels).astype(F32)
    hit3 = jnp.where(
        iota((devices, anchors_dev, pixels), 2).astype(F32) == pos_local, 1.0, 0.0
    )
    hit = hit3.reshape(anchors_all, pixels).astype(BF16)

    others(from_all(qall, q_send, q_recv))
    queries = qall[...].reshape(anchors_all, LANES)
    exp_scores = jnp.exp(mm(keys, queries, NT) / SOFTMAX_TEMPER)
    part_total = jnp.sum(exp_scores, axis=0, keepdims=True)
    part_pos = mm(hit, keys, NN)
    pos_sum = jnp.sum(
        jnp.sum(part_pos * queries.astype(F32), axis=1, keepdims=True), axis=0, keepdims=True
    )
    tot_rows = anchors_all // LANES
    rows = [part_total[:, r * LANES : (r + 1) * LANES] for r in range(tot_rows)]
    rows.append(jnp.broadcast_to(pos_sum, (1, LANES)))
    for r in range(tot_rows + 1):
        totp[r : r + 1, :] = rows[r]
    tot_pair = remote(totp, totx, totx_send, totx_recv, partner)
    tot_pair.start()
    part_weighted = mm(exp_scores.astype(BF16), keys, TN)
    by_owner = part_weighted.reshape(chips, 2, anchors_dev, LANES).astype(BF16)
    pos_owner = part_pos.reshape(chips, 2, anchors_dev, LANES).astype(BF16)
    for half in range(2):
        wps[half, :, :anchors_dev, :] = by_owner[:, half]
        wps[half, :, anchors_dev:, :] = pos_owner[:, half]
    part_pair = remote(wps.at[1 - core], wpx, wpx_send, wpx_recv, partner)
    part_pair.start()
    tot_pair.wait()
    totb[chip] = totp[...] + totx[...]

    def send_total(target):
        remote(
            totb.at[chip],
            totb.at[chip],
            tot_send.at[target],
            tot_recv.at[chip],
            target * 2 + core,
        ).start()

    other_chips(send_total)
    part_pair.wait()
    wpc[...] = (wps[core].astype(F32) + wpx[...].astype(F32)).astype(BF16)

    def send_part(target):
        remote(
            wpc.at[target], wpr.at[chip], wp_send.at[target], wp_recv.at[chip], target * 2 + core
        ).start()

    other_chips(send_part)
    wpr[chip] = wpc[chip]
    pushed = mm(hit, queries, TN)

    def total_done(source):
        copy = remote(
            totb.at[source],
            totb.at[source],
            tot_send.at[source],
            tot_recv.at[source],
            source * 2 + core,
        )
        copy.wait_recv()
        copy.wait_send()

    other_chips(total_done)
    sums = jnp.sum(totb[...], axis=0)
    total_row = jnp.concatenate([sums[r : r + 1, :] for r in range(tot_rows)], axis=1)
    loss = jnp.sum(jnp.log(total_row), axis=1, keepdims=True) - sums[
        tot_rows : tot_rows + 1, 0:1
    ] / SOFTMAX_TEMPER
    loss_ref[...] = loss / anchor_count
    inverse = (1.0 / total_row).astype(BF16).astype(F32)
    soft = (exp_scores * inverse).astype(BF16)
    pulled = mm(soft, queries, NN)
    mine = iota((anchors_dev, anchors_all), 1) == me * anchors_dev + iota(
        (anchors_dev, anchors_all), 0
    )
    own_total = jnp.sum(jnp.where(mine, total_row, 0.0), axis=1, keepdims=True)

    def part_done(source):
        copy = remote(
            wpc.at[source], wpr.at[source], wp_send.at[source], wp_recv.at[source], source * 2 + core
        )
        copy.wait_recv()
        copy.wait_send()

    other_chips(part_done)
    both = jnp.sum(wpr[...].astype(F32), axis=0)
    grad_query = (both[:anchors_dev] / own_total - both[anchors_dev:]) * gradient_scale
    grad_key = gradient_scale * (pulled - pushed)
    grad_key = grad_key + mm(pick, grad_query, TN, lax.Precision.HIGHEST)
    along = jnp.sum(grad_key * unit_key, axis=1, keepdims=True)
    grad_raw = ((grad_key - unit_key * along) / norm_key).astype(BF16)
    grad_mixed = mm(grad_raw, proj_ref[...], NT).astype(BF16)
    gm[...] = grad_mixed
    gp[...] = (grad_mixed.astype(F32) * slope[...]).astype(BF16)
    g_halo = halo(gp, gh, gh_send, gh_recv)
    halo_start(g_halo)

    gpj[...] = mm(mixed_t[...], grad_raw, NN)
    lane_group = iota((group, LANES), 1) // group

    def weight_grad(b, carry):
        lane = pl.ds(pl.multiple_of(b * LANES, LANES), LANES)
        full = mm(at[b], gp[:, lane], NN)
        for tap in range(tap_count):
            folded = jnp.zeros((group, LANES), F32)
            for g in range(per_block):
                first = tap * LANES + g * group
                folded = jnp.where(lane_group == g, full[first : first + group], folded)
            gw[b, tap * group : (tap + 1) * group, :] = folded
        return carry

    lax.fori_loop(0, blocks, weight_grad, 0)
    if gw.shape[1] > tap_count * group:
        gw[:, tap_count * group :, :] = jnp.zeros(
            (blocks, gw.shape[1] - tap_count * group, LANES), F32
        )

    def chunk(half, i):
        b = half * (blocks // 2) + i // pieces
        first = pl.multiple_of(lax.rem(i, pieces) * piece, 8)
        first_p = pl.multiple_of((half * chips + i) * prow, 8)
        return gpj[pl.ds(first_p, prow), :], gw[b, pl.ds(first, piece), :]

    def fill(i, carry):
        proj_part, conv_part = chunk(1 - core, i)
        l1s[i, :prow, :] = proj_part.astype(BF16)
        l1s[i, prow:, :] = conv_part.astype(BF16)
        return carry

    lax.fori_loop(0, chips, fill, 0)
    l1 = remote(l1s, l1r, l1_send, l1_recv, partner)
    l1.start()
    store_shifted(gs, pixels, cols, gp[...], cols)
    l1.wait()

    def join(i, carry):
        proj_part, conv_part = chunk(core, i)
        l2s[i, :prow, :] = (proj_part + l1r[i, :prow, :].astype(F32)).astype(BF16)
        l2s[i, prow:, :] = (conv_part + l1r[i, prow:, :].astype(F32)).astype(BF16)
        return carry

    lax.fori_loop(0, chips, join, 0)

    def send_chunk(target):
        remote(
            l2s.at[target],
            l2r.at[chip],
            l2_send.at[target],
            l2_recv.at[chip],
            target * 2 + core,
        ).start()

    other_chips(send_chunk)
    l2r[chip] = l2s[chip]

    halo_wait(g_halo, gh)
    store_shifted(gs, cols, 0, gh[0], cols)
    store_shifted(gs, cols, cols + pixels, gh[1], cols)

    def backward(b, carry):
        lane = pl.ds(pl.multiple_of(b * LANES, LANES), LANES)
        back = mm(windows(gs, lane, True), wt[b], NT).astype(BF16)
        out_ref[:, lane] = (back.astype(F32) + gm[:, lane].astype(F32)).astype(BF16)
        return carry

    lax.fori_loop(0, blocks, backward, 0)

    def chunk_done(source):
        copy = remote(
            l2s.at[source],
            l2r.at[source],
            l2_send.at[source],
            l2_recv.at[source],
            source * 2 + core,
        )
        copy.wait_recv()
        copy.wait_send()

    other_chips(chunk_done)
    ag[core, chip] = jnp.sum(l2r[...].astype(F32), axis=0).astype(BF16)

    place = lax.rem(chip, inner)
    layer = chip // inner
    layers = chips // inner

    def chunk_copy(index, send_sem, target):
        return remote(
            ag.at[core, index], ag.at[core, index], send_sem, ag_recv.at[index], target
        )

    def pair_copy(index, half):
        return remote(
            ag.at[half, index],
            ag.at[half, index],
            pair_send.at[index],
            pair_recv.at[index],
            partner,
        )

    def far_copy(target):
        return chunk_copy(chip, ag_send.at[target], (target * inner + place) * 2 + core)

    def near_copy(source, target):
        return chunk_copy(
            source * inner + place, near_send.at[source, target], (layer * inner + target) * 2 + core
        )

    def turn(count, start, body):
        def step(k, carry):
            body(lax.rem(start + k, count))
            return carry

        lax.fori_loop(1, count, step, 0)

    def forward_near(source):
        turn(inner, place, lambda target: near_copy(source, target).start())
        pair_copy(source * inner + place, core).start()

    turn(layers, layer, lambda target: far_copy(target).start())
    forward_near(layer)

    def far_arrived(source):
        chunk_copy(source * inner + place, ag_send.at[source], partner).wait_recv()
        forward_near(source)

    turn(layers, layer, far_arrived)

    def near_arrived(k, carry):
        source = lax.rem(layer + k, layers)

        def one(other):
            index = source * inner + other
            chunk_copy(index, near_send.at[source, other], partner).wait_recv()
            pair_copy(index, core).start()

        turn(inner, place, one)
        return carry

    lax.fori_loop(0, layers, near_arrived, 0)

    turn(layers, layer, lambda target: far_copy(target).wait_send())

    def near_sent(source, carry):
        turn(inner, place, lambda target: near_copy(source, target).wait_send())
        return carry

    lax.fori_loop(0, layers, near_sent, 0)

    def pair_done(i, carry):
        pair_copy(i, core).wait_send()
        pair_copy(i, 1 - core).wait_recv()
        return carry

    lax.fori_loop(0, chips, pair_done, 0)


def finish(geometry, gf_ref, ag, loss_ref, gf_out, gw_out, gp_out, loss_out):
    blocks, chips, pieces, piece, prow = geometry
    gf_out[...] = gf_ref[...]
    loss_out[...] = loss_ref[...]
    height = gw_out.shape[0]
    for half in range(2):
        for i in range(chips):
            b = half * (blocks // 2) + i // pieces
            first = i % pieces * piece
            first_p = (half * chips + i) * prow
            keep = min(piece, height - first)
            gp_out[first_p : first_p + prow, :] = ag[half, i, :prow, :].astype(F32)
            if keep > 0:
                gw_out[first : first + keep, b * LANES : (b + 1) * LANES] = ag[
                    half, i, prow : prow + keep, :
                ].astype(F32)


def per_device(devices, batches, features, conv_weight, proj_weight, anchor_pixel, positive_pixel):
    rows_dev, cols, images, channels = features.shape
    group = conv_weight.shape[2]
    key_width = proj_weight.shape[1]
    anchors_dev = anchor_pixel.shape[0]
    inner = min(4, devices // 2)
    pixels = rows_dev * cols
    taps = conv_weight.shape[0] * conv_weight.shape[1]
    blocks = channels // LANES
    chips = devices // 2
    pieces = chips // (blocks // 2)
    piece = -(-(taps * group) // pieces)
    piece = -(-piece // 8) * 8
    prow = channels // devices
    anchors_all = anchors_dev * devices
    anchor_count = anchors_all * images * batches
    gradient_scale = 1.0 / (SOFTMAX_TEMPER * anchor_count)
    tot_rows = anchors_all // LANES + 1
    padded = pixels + 2 * cols
    dma = pltpu.SemaphoreType.DMA
    chunk_rows = prow + piece
    vmem = pltpu.VMEM
    whole = pl.BlockSpec(memory_space=pltpu.VMEM)
    scratch = [
        vmem((2, cols, channels), BF16),
        vmem((3, padded, channels), BF16),
        vmem((blocks, taps * LANES, LANES), BF16),
        vmem((blocks, LANES, taps * LANES), BF16),
        vmem((blocks, taps * LANES, pixels), BF16),
        vmem((pixels, channels), BF16),
        vmem((channels, pixels), BF16),
        vmem((pixels, channels), F32),
        vmem((devices, 1, LANES), F32),
        vmem((devices, anchors_dev, LANES), BF16),
        vmem((tot_rows, LANES), F32),
        vmem((tot_rows, LANES), F32),
        vmem((chips, tot_rows, LANES), F32),
        vmem((2, chips, 2 * anchors_dev, LANES), BF16),
        vmem((chips, 2 * anchors_dev, LANES), BF16),
        vmem((chips, 2 * anchors_dev, LANES), BF16),
        vmem((chips, 2 * anchors_dev, LANES), BF16),
        vmem((pixels, channels), BF16),
        vmem((pixels, channels), BF16),
        vmem((2, cols, channels), BF16),
        vmem((3, padded, channels), BF16),
        vmem((blocks, pieces * piece, LANES), F32),
        vmem((channels, LANES), F32),
        vmem((chips, chunk_rows, LANES), BF16),
        vmem((chips, chunk_rows, LANES), BF16),
        vmem((chips, chunk_rows, LANES), BF16),
        vmem((chips, chunk_rows, LANES), BF16),
        dma((2,)),
        dma((2,)),
        dma((2,)),
        dma((2,)),
    ]
    scratch += [dma((devices,))] * 4
    scratch += [dma((chips,))] * 4
    scratch += [dma] * 4
    scratch += [dma, dma]
    scratch += [dma((chips,))] * 2
    scratch += [dma((chips // inner,)), dma((chips // inner, inner))]
    scratch += [dma((chips,))] * 3
    sums = (
        jax.ShapeDtypeStruct((pixels, channels), BF16),
        jax.ShapeDtypeStruct((2, chips, chunk_rows, LANES), BF16),
        jax.ShapeDtypeStruct((1, 1), F32),
    )
    parts = pl.pallas_call(
        functools.partial(
            kernel,
            devices,
            anchors_all,
            gradient_scale,
            (cols, group, pieces, piece, prow, inner, anchor_count),
        ),
        out_shape=sums,
        in_specs=[whole] * 5,
        out_specs=(whole,) * 3,
        scratch_shapes=scratch,
        compiler_params=pltpu.CompilerParams(
            collective_id=0, has_side_effects=True, vmem_limit_bytes=40000 * 1024
        ),
    )(
        features.reshape(pixels, channels),
        conv_weight.reshape(taps, group, channels),
        proj_weight,
        anchor_pixel.reshape(1, anchors_dev),
        positive_pixel.reshape(1, anchors_dev),
    )
    grad_features, grad_conv, grad_proj, loss = pl.pallas_call(
        functools.partial(finish, (blocks, chips, pieces, piece, prow)),
        out_shape=(
            jax.ShapeDtypeStruct((pixels, channels), BF16),
            jax.ShapeDtypeStruct((taps * group, channels), F32),
            jax.ShapeDtypeStruct((channels, key_width), F32),
            jax.ShapeDtypeStruct((1, 1), F32),
        ),
        in_specs=[whole] * 3,
        out_specs=(whole,) * 4,
        compiler_params=pltpu.CompilerParams(vmem_limit_bytes=16000 * 1024),
    )(*parts)
    grad_conv = grad_conv.reshape(conv_weight.shape)
    loss_value = loss.reshape(())
    if batches > 1:
        grad_conv, grad_proj, loss_value = lax.psum((grad_conv, grad_proj, loss_value), "batch")
    return (grad_features.reshape(features.shape), grad_conv, grad_proj, loss_value)


def solution(mesh):
    placed = (P("wide", None, "batch", None), P(), P(), P("wide", "batch"), P("wide", "batch"))
    return jax.shard_map(
        functools.partial(per_device, mesh.shape["wide"], mesh.shape["batch"]),
        mesh=mesh,
        in_specs=placed,
        out_specs=(P("wide", None, "batch", None), P(), P(), P()),
        check_vma=False,
    )
```

profile of v0, /device:TPU:0, one launch (start us, length us, event | category | flops | bytes accessed | tf_op | source)
XLA Modules:
  0.0 63.5 jit_solution(5342818073951132211)
XLA Ops:
  0.6 0.0 copy-start
  0.6 1.1 %copy-done = bf16[3,3,32,1024]{3,2,1,0:T(8,128)(2,1)S(1)} copy-done((bf16[3,3,32,1024]{3,2,1,0:T(8,128)(2,1)S(1)}, bf16[3,3,32,1024]{3,2,1,0:T(8,128)(2,1)}, u32[]{:S(2)}) %copy-start) | copy-done | bytes 589848
  1.7 0.0 copy-start.1
  1.7 0.9 %copy-done.1 = bf16[2,64,1,1024]{3,1,2,0:T(8,128)(2,1)S(1)} copy-done((bf16[2,64,1,1024]{3,1,2,0:T(8,128)(2,1)S(1)}, bf16[2,64,1,1024]{3,1,2,0:T(8,128)(2,1)}, u32[]{:S(2)}) %copy-start.1) | copy-done | bytes 262168
  2.6 0.0 copy-start.2
  2.6 0.9 %copy-done.2 = bf16[1024,128]{1,0:T(8,128)(2,1)S(1)} copy-done((bf16[1024,128]{1,0:T(8,128)(2,1)S(1)}, bf16[1024,128]{1,0:T(8,128)(2,1)}, u32[]{:S(2)}) %copy-start.2) | copy-done | bytes 262168
  3.6 0.0 copy-start.3
  3.6 0.7 %copy-done.3 = s32[16,1]{0,1:T(1,128)S(1)} copy-done((s32[16,1]{0,1:T(1,128)S(1)}, s32[16,1]{0,1:T(1,128)}, u32[]{:S(2)}) %copy-start.3) | copy-done | bytes 88
  4.3 0.0 copy-start.4
  4.3 0.7 %copy-done.4 = s32[16,1]{0,1:T(1,128)S(1)} copy-done((s32[16,1]{0,1:T(1,128)S(1)}, s32[16,1]{0,1:T(1,128)}, u32[]{:S(2)}) %copy-start.4) | copy-done | bytes 88
  4.9 56.5 %shard_map.84 = (bf16[128,1024]{1,0:T(8,128)(2,1)S(1)}, bf16[2,16,104,128]{3,2,1,0:T(8,128)(2,1)S(1)}, f32[1,1]{1,0:T(1,128)}) custom-call(bf16[128,1024]{1,0:T(8,128)(2,1)S(1)} %bitcast.10, bf16[9,32,1024]{2,1,0:T(8,128)(2,1)S(1)} %bitcast.9, bf16[1024,128]{1,0:T(8,128)(2,1)S(1)} %copy-done.2, s32[1,16]{1,0:T(1,128)S(1)} %bitcast.11, s32[1,16]{1,0:T(1,128)S(1)} %bitcast.12), custom_call_target="tpu_custom_call" | custom-call | tf_op jit(solution)/shard_map/pallas_call | solution.py:633
  61.4 2.1 %shard_map.85 = (bf16[128,1024]{1,0:T(8,128)(2,1)}, f32[288,1024]{1,0:T(8,128)}, f32[1024,128]{1,0:T(8,128)}, f32[1,1]{1,0:T(1,128)}) custom-call(bf16[128,1024]{1,0:T(8,128)(2,1)S(1)} %get-tuple-element.11.gf_ref, bf16[2,16,104,128]{3,2,1,0:T(8,128)(2,1)S(1)} %get-tuple-element.12.ag, f32[1,1]{1,0:T(1,128)} %get-tuple-element.13.loss_ref), custom_call_target="tpu_custom_call" | custom-call | tf_op jit(solution)/shard_map/pallas_call | solution.py:655
Async XLA Ops:
  0.6 1.1 %copy-start = (bf16[3,3,32,1024]{3,2,1,0:T(8,128)(2,1)S(1)}, bf16[3,3,32,1024]{3,2,1,0:T(8,128)(2,1)}, u32[]{:S(2)}) copy-start(bf16[3,3,32,1024]{3,2,1,0:T(8,128)(2,1)} %param.6) | copy-start | bytes 1769476
  1.7 0.9 %copy-start.1 = (bf16[2,64,1,1024]{3,1,2,0:T(8,128)(2,1)S(1)}, bf16[2,64,1,1024]{3,1,2,0:T(8,128)(2,1)}, u32[]{:S(2)}) copy-start(bf16[2,64,1,1024]{3,1,2,0:T(8,128)(2,1)} %param.5) | copy-start | bytes 786436
  2.6 0.9 %copy-start.2 = (bf16[1024,128]{1,0:T(8,128)(2,1)S(1)}, bf16[1024,128]{1,0:T(8,128)(2,1)}, u32[]{:S(2)}) copy-start(bf16[1024,128]{1,0:T(8,128)(2,1)} %proj_ref.1) | copy-start | bytes 786436
  3.6 0.7 %copy-start.3 = (s32[16,1]{0,1:T(1,128)S(1)}, s32[16,1]{0,1:T(1,128)}, u32[]{:S(2)}) copy-start(s32[16,1]{0,1:T(1,128)} %param.8) | copy-start | bytes 196
  4.3 0.7 %copy-start.4 = (s32[16,1]{0,1:T(1,128)S(1)}, s32[16,1]{0,1:T(1,128)}, u32[]{:S(2)}) copy-start(s32[16,1]{0,1:T(1,128)} %param.9) | copy-start | bytes 196
where the time goes:
time: 63.8 us; the launch traced here: 63.5 us
  Pallas kernels  58.6 us (92%)
  local copies, waits for them, and re-layouts  4.27 us (7%)
  between operations  0.65 us (1%)
    pallas_call x1, Pallas kernels, per_device(): pl.pallas_call(functools.partial(kernel, devices, anchors_all, gradient_s...  56.5 us
    unnamed x10, local copies, waits for them, and re-layouts  4.27 us
    pallas_call x1, Pallas kernels, per_device(): pl.pallas_call(functools.partial(finish, (blocks, chips, pieces, piece, p...  2.12 us

commit v1 on v0

--- a/solution.py
+++ b/solution.py
@@ -43,14 +43,18 @@
     anchors_all,
     gradient_scale,
     geometry,
-    x_ref,
-    w_ref,
-    proj_ref,
+    x_hbm,
+    w_hbm,
+    proj_hbm,
     anchor_ref,
     positive_ref,
     out_ref,
     ag,
     loss_ref,
+    x_ref,
+    w_ref,
+    proj_ref,
+    load,
     xh,
     xs,
     wn,
@@ -78,6 +82,8 @@
     l1r,
     l2s,
     l2r,
+    l3s,
+    l3r,
     xh_send,
     xh_recv,
     gh_send,
@@ -98,6 +104,8 @@
     l1_recv,
     l2_send,
     l2_recv,
+    l3_send,
+    l3_recv,
     ag_send,
     near_send,
     ag_recv,
@@ -114,6 +122,9 @@
     core = lax.rem(me, 2)
     chip = me // 2
     partner = me + 1 - 2 * core
+    place = lax.rem(chip, inner)
+    layer = chip // inner
+    layers = chips // inner
     barrier = pltpu.get_barrier_semaphore()
 
     def others(body):
@@ -122,6 +133,21 @@
             return carry
 
         lax.fori_loop(1, devices, step, 0)
+
+    def turn(count, start, body):
+        def step(k, carry):
+            body(lax.rem(start + k, count))
+            return carry
+
+        lax.fori_loop(1, count, step, 0)
+
+    def block_loop(start, stop, body):
+        def step(i, carry):
+            for j in range(2):
+                body(2 * i + j, carry)
+            return carry
+
+        lax.fori_loop(start // 2, stop // 2, step, 0)
 
     def other_chips(body):
         def step(k, carry):
@@ -143,7 +169,17 @@
     def signal_entry(target):
         pl.semaphore_signal(barrier, inc=1, device_id={"wide": target}, device_id_type=MESH)
 
+    loads = [
+        pltpu.make_async_copy(src, dst, load.at[n])
+        for n, (src, dst) in enumerate(
+            ((w_hbm, w_ref), (x_hbm, x_ref), (proj_hbm, proj_ref))
+        )
+    ]
+    for copy in loads:
+        copy.start()
     others(signal_entry)
+    for copy in loads:
+        copy.wait()
 
     tap_count = w_ref.shape[0]
     diagonal = iota((LANES, LANES), 0) // group == iota((LANES, LANES), 1) // group
@@ -261,7 +297,7 @@
         slope[:, lane] = sig * (1.0 + pre * (1.0 - sig))
         return carry
 
-    lax.fori_loop(0, blocks, forward, 0)
+    block_loop(0, blocks, forward)
 
     raw_key = mm(mixed[...], proj_ref[...], NN)
     norm_key = jnp.sqrt(jnp.sum(raw_key * raw_key, axis=1, keepdims=True) + EPSILON)
@@ -280,7 +316,7 @@
         mixed_t[lane, :] = mixed[:, lane].T
         return carry
 
-    lax.fori_loop(0, blocks, flip_over, 0)
+    block_loop(0, blocks, flip_over)
 
     others(from_all(posb, pos_send, pos_recv))
     own_lane = iota((devices, anchors_dev, LANES), 1) == iota((devices, anchors_dev, LANES), 2)
@@ -399,7 +435,7 @@
             gw[b, tap * group : (tap + 1) * group, :] = folded
         return carry
 
-    lax.fori_loop(0, blocks, weight_grad, 0)
+    block_loop(0, blocks, weight_grad)
     if gw.shape[1] > tap_count * group:
         gw[:, tap_count * group :, :] = jnp.zeros(
             (blocks, gw.shape[1] - tap_count * group, LANES), F32
@@ -425,23 +461,33 @@
 
     def join(i, carry):
         proj_part, conv_part = chunk(core, i)
-        l2s[i, :prow, :] = (proj_part + l1r[i, :prow, :].astype(F32)).astype(BF16)
-        l2s[i, prow:, :] = (conv_part + l1r[i, prow:, :].astype(F32)).astype(BF16)
+        to, at_layer = lax.rem(i, inner), i // inner
+        l2s[to, at_layer, :prow, :] = (proj_part + l1r[i, :prow, :].astype(F32)).astype(BF16)
+        l2s[to, at_layer, prow:, :] = (conv_part + l1r[i, prow:, :].astype(F32)).astype(BF16)
         return carry
 
     lax.fori_loop(0, chips, join, 0)
 
-    def send_chunk(target):
-        remote(
+    def near_sum(target, slot):
+        return remote(
             l2s.at[target],
-            l2r.at[chip],
+            l2r.at[slot],
             l2_send.at[target],
-            l2_recv.at[chip],
-            target * 2 + core,
-        ).start()
-
-    other_chips(send_chunk)
-    l2r[chip] = l2s[chip]
+            l2_recv.at[slot],
+            (layer * inner + target) * 2 + core,
+        )
+
+    def far_sum(target, slot):
+        return remote(
+            l3s.at[target],
+            l3r.at[slot],
+            l3_send.at[target],
+            l3_recv.at[slot],
+            (target * inner + place) * 2 + core,
+        )
+
+    turn(inner, place, lambda target: near_sum(target, place).start())
+    l2r[place] = l2s[place]
 
     halo_wait(g_halo, gh)
     store_shifted(gs, cols, 0, gh[0], cols)
@@ -453,25 +499,26 @@
         out_ref[:, lane] = (back.astype(F32) + gm[:, lane].astype(F32)).astype(BF16)
         return carry
 
-    lax.fori_loop(0, blocks, backward, 0)
-
-    def chunk_done(source):
-        copy = remote(
-            l2s.at[source],
-            l2r.at[source],
-            l2_send.at[source],
-            l2_recv.at[source],
-            source * 2 + core,
-        )
+    block_loop(0, blocks // 2, backward)
+
+    def near_done(source):
+        copy = near_sum(source, source)
         copy.wait_recv()
         copy.wait_send()
 
-    other_chips(chunk_done)
-    ag[core, chip] = jnp.sum(l2r[...].astype(F32), axis=0).astype(BF16)
-
-    place = lax.rem(chip, inner)
-    layer = chip // inner
-    layers = chips // inner
+    def far_done(source):
+        copy = far_sum(source, source)
+        copy.wait_recv()
+        copy.wait_send()
+
+    turn(inner, place, near_done)
+    for z in range(layers):
+        l3s[z] = jnp.sum(l2r[:, z].astype(F32), axis=0).astype(BF16)
+    turn(layers, layer, lambda target: far_sum(target, layer).start())
+    l3r[layer] = l3s[layer]
+    block_loop(blocks // 2, blocks, backward)
+    turn(layers, layer, far_done)
+    ag[core, chip] = jnp.sum(l3r[...].astype(F32), axis=0).astype(BF16)
 
     def chunk_copy(index, send_sem, target):
         return remote(
@@ -494,13 +541,6 @@
         return chunk_copy(
             source * inner + place, near_send.at[source, target], (layer * inner + target) * 2 + core
         )
-
-    def turn(count, start, body):
-        def step(k, carry):
-            body(lax.rem(start + k, count))
-            return carry
-
-        lax.fori_loop(1, count, step, 0)
 
     def forward_near(source):
         turn(inner, place, lambda target: near_copy(source, target).start())
@@ -568,6 +608,7 @@
     key_width = proj_weight.shape[1]
     anchors_dev = anchor_pixel.shape[0]
     inner = min(4, devices // 2)
+    layers = devices // 2 // inner
     pixels = rows_dev * cols
     taps = conv_weight.shape[0] * conv_weight.shape[1]
     blocks = channels // LANES
@@ -586,6 +627,10 @@
     vmem = pltpu.VMEM
     whole = pl.BlockSpec(memory_space=pltpu.VMEM)
     scratch = [
+        vmem((pixels, channels), BF16),
+        vmem((taps, group, channels), BF16),
+        vmem((channels, key_width), BF16),
+        dma((3,)),
         vmem((2, cols, channels), BF16),
         vmem((3, padded, channels), BF16),
         vmem((blocks, taps * LANES, LANES), BF16),
@@ -611,8 +656,10 @@
         vmem((channels, LANES), F32),
         vmem((chips, chunk_rows, LANES), BF16),
         vmem((chips, chunk_rows, LANES), BF16),
-        vmem((chips, chunk_rows, LANES), BF16),
-        vmem((chips, chunk_rows, LANES), BF16),
+        vmem((inner, layers, chunk_rows, LANES), BF16),
+        vmem((inner, layers, chunk_rows, LANES), BF16),
+        vmem((layers, chunk_rows, LANES), BF16),
+        vmem((layers, chunk_rows, LANES), BF16),
         dma((2,)),
         dma((2,)),
         dma((2,)),
@@ -622,8 +669,9 @@
     scratch += [dma((chips,))] * 4
     scratch += [dma] * 4
     scratch += [dma, dma]
-    scratch += [dma((chips,))] * 2
-    scratch += [dma((chips // inner,)), dma((chips // inner, inner))]
+    scratch += [dma((inner,))] * 2
+    scratch += [dma((layers,))] * 2
+    scratch += [dma((layers,)), dma((layers, inner))]
     scratch += [dma((chips,))] * 3
     sums = (
         jax.ShapeDtypeStruct((pixels, channels), BF16),
@@ -639,11 +687,11 @@
             (cols, group, pieces, piece, prow, inner, anchor_count),
         ),
         out_shape=sums,
-        in_specs=[whole] * 5,
+        in_specs=[pl.BlockSpec(memory_space=pltpu.HBM)] * 3 + [whole] * 2,
         out_specs=(whole,) * 3,
         scratch_shapes=scratch,
         compiler_params=pltpu.CompilerParams(
-            collective_id=0, has_side_effects=True, vmem_limit_bytes=40000 * 1024
+            collective_id=0, has_side_effects=True, vmem_limit_bytes=65000 * 1024
         ),
     )(
         features.reshape(pixels, channels),
@@ -662,7 +710,7 @@
         ),
         in_specs=[whole] * 3,
         out_specs=(whole,) * 4,
-        compiler_params=pltpu.CompilerParams(vmem_limit_bytes=16000 * 1024),
+        compiler_params=pltpu.CompilerParams(vmem_limit_bytes=65000 * 1024),
     )(*parts)
     grad_conv = grad_conv.reshape(conv_weight.shape)
     loss_value = loss.reshape(())

time: 63.8 us -> 58.6 us (0.918)
  local copies, waits for them, and re-layouts: 4.27 us -> 0 us
  Pallas kernels: 58.6 us -> 57.7 us
    unnamed x10 -> x0, local copies, waits for them, and re-layouts: 4.27 us -> none
    pallas_call x1, Pallas kernels: 56.5 us -> 54.4 us  [per_device(): pl.pallas_call(functools.partial(kernel, devices, anchors_all, gradient_s...]
    pallas_call x1, Pallas kernels: 2.12 us -> 3.29 us  [per_device(): pl.pallas_call(functools.partial(finish, (blocks, chips, pieces, piece, p...]
where the time goes in v1:
time: 58.6 us; the launch traced here: 58.4 us
  Pallas kernels  57.7 us (98%)
  between operations  0.64 us (1%)
    pallas_call x1, Pallas kernels, per_device(): pl.pallas_call(functools.partial(kernel, devices, anchors_all, gradient_s...  54.4 us
    pallas_call x1, Pallas kernels, per_device(): pl.pallas_call(functools.partial(finish, (blocks, chips, pieces, piece, p...  3.29 us

profile of v1, /device:TPU:0, one launch (start us, length us, event | category | flops | bytes accessed | tf_op | source)
XLA Modules:
  0.0 58.4 jit_solution(4020214903513289315)
XLA Ops:
  0.6 54.4 %shard_map.84 = (bf16[128,1024]{1,0:T(8,128)(2,1)}, bf16[2,16,104,128]{3,2,1,0:T(8,128)(2,1)}, f32[1,1]{1,0:T(1,128)}) custom-call(bf16[128,1024]{1,0:T(8,128)(2,1)} %bitcast.10, bf16[9,32,1024]{2,1,0:T(8,128)(2,1)} %bitcast.9, bf16[1024,128]{1,0:T(8,128)(2,1)} %proj_hbm.1, s32[1,16]{1,0:T(1,128)} %bitcast.11, s32[1,16]{1,0:T(1,128)} %bitcast.12), custom_call_target="tpu_custom_call" | custom-call | tf_op jit(solution)/shard_map/pallas_call | solution.py:681
  55.1 3.3 %shard_map.85 = (bf16[128,1024]{1,0:T(8,128)(2,1)}, f32[288,1024]{1,0:T(8,128)}, f32[1024,128]{1,0:T(8,128)}, f32[1,1]{1,0:T(1,128)}) custom-call(bf16[128,1024]{1,0:T(8,128)(2,1)} %get-tuple-element.11.gf_ref, bf16[2,16,104,128]{3,2,1,0:T(8,128)(2,1)} %get-tuple-element.12.ag, f32[1,1]{1,0:T(1,128)} %get-tuple-element.13.loss_ref), custom_call_target="tpu_custom_call" | custom-call | tf_op jit(solution)/shard_map/pallas_call | solution.py:703
